TPU v7x, 32 devices: a whole 2x2x4 slice. The times are simulated.
32 devices in a mesh: dp: 16 (over z, y, x), group: 2 (over core).
Axes of the slice: x: 2, y: 2, z: 4, core: 2. Of those that a mesh axis runs over, the one named last changes fastest.
Arguments:
- acts_first: bfloat16 [32, 32, 32, 256], P(('dp', 'group'))
- grads_first: bfloat16 [32, 32, 32, 256], P(('dp', 'group'))
- acts_second: bfloat16 [32, 32, 32, 256], P(('dp', 'group'))
- grads_second: bfloat16 [32, 16, 16, 256], P(('dp', 'group'))
- grad_w: bfloat16 [2, 256, 2304], P(None, 'dp'), may hold values from -6 to 6
- owner: int32 [2], replicated, may hold values from 0 to 7, as said below
- basis_in: bfloat16 [8, 256, 256], P('group'), may hold values from -0.375 to 0.375
- basis_spatial: bfloat16 [8, 9, 9], P('group'), may hold values from -2 to 2
- basis_out: bfloat16 [8, 256, 256], P('group'), may hold values from -0.375 to 0.375
Outputs:
- precond: bfloat16 [2, 256, 2304], P(None, 'dp')
- factor_in: float32 [2, 256, 256], replicated
- factor_spatial: float32 [2, 9, 9], replicated
- factor_out: float32 [2, 256, 256], replicated
Inputs may be any that keep to these rules, and one draw needn't show every extreme that they name: owner[l] is the slot that holds layer l's bases, one of the 4 slots of group owner[l] // 4; no two layers share a slot.
All inputs are finite; a program needn't handle non-finite values.
Results may differ from a plain program's by a relative error of at most 0.0045.
Values may be sent and summed in bfloat16 or wider, within the bound.
A program may use at most 64 MiB of HBM per device.

v0:
```python
import jax
import jax.numpy as jnp
from jax import lax
from jax.sharding import PartitionSpec as P

LAYERS = 2


DAMPING = 0.1


def from_root(block, axis, holder):
    block = jnp.where(lax.axis_index(axis) == holder, block, jnp.zeros_like(block))
    return lax.psum(block, axis)


def window_views(images, stride, out_side):
    padded = jnp.pad(images, ((0, 0), (1, 1), (1, 1), (0, 0)))
    extent = stride * (out_side - 1) + 1
    limit_n = images.shape[0]
    channels = images.shape[3]
    windows = []
    for row_off in range(3):
        for col_off in range(3):
            windows.append(
                lax.slice(
                    padded,
                    (0, row_off, col_off, 0),
                    (limit_n, row_off + extent, col_off + extent, channels),
                    (1, stride, stride, 1),
                )
            )
    return jnp.stack(windows)


def gram_terms(images, grads_out, stride):
    stacked = window_views(images, stride, grads_out.shape[1])
    channels = images.shape[3]
    patch_rows = stacked.reshape(-1, channels)
    channel_sum = lax.dot_general(
        patch_rows, patch_rows, (((0,), (0,)), ((), ())), preferred_element_type=jnp.float32
    )
    tap_rows = stacked.reshape(9, -1)
    spatial_sum = lax.dot_general(
        tap_rows, tap_rows, (((1,), (1,)), ((), ())), preferred_element_type=jnp.float32
    )
    out_rows = grads_out.reshape(-1, channels)
    output_sum = lax.dot_general(
        out_rows, out_rows, (((0,), (0,)), ((), ())), preferred_element_type=jnp.float32
    )
    return (channel_sum, spatial_sum, output_sum)


def eigen_values(basis, factor):
    basis_f = basis.astype(jnp.float32)
    return jnp.sum(basis_f * jnp.dot(factor, basis_f, precision=lax.Precision.HIGHEST), axis=0)


def rotated_grad(weights, basis_chan, basis_tap):
    outs_n, taps_n, chans_n = weights.shape
    inner_in = jnp.dot(
        weights.reshape(outs_n * taps_n, chans_n), basis_chan, preferred_element_type=jnp.float32
    ).reshape(outs_n, taps_n, -1)
    turned = jnp.einsum(
        "okj,kl->olj", inner_in, basis_tap.astype(jnp.float32), precision=lax.Precision.HIGHEST
    )
    return turned.astype(jnp.bfloat16)


def scaled_coords(rotated, basis_outc, scale_out, scale_tap, scale_in):
    chans_out = basis_outc.shape[0]
    projected = lax.dot_general(
        basis_outc,
        rotated.reshape(chans_out, -1),
        (((0,), (0,)), ((), ())),
        preferred_element_type=jnp.float32,
    ).reshape(rotated.shape)
    divisor = (
        scale_out[:, None, None] * scale_tap[None, :, None] * scale_in[None, None, :] + DAMPING
    )
    return (projected / divisor).astype(jnp.bfloat16)


def back_rows(coords, rows_basis, basis_chan, basis_tap):
    row_n = rows_basis.shape[0]
    col_n = coords.shape[2]
    turned_back = jnp.dot(
        rows_basis, coords.reshape(coords.shape[0], -1), preferred_element_type=jnp.float32
    ).astype(jnp.bfloat16)
    chan_back = lax.dot_general(
        turned_back.reshape(row_n * 9, col_n),
        basis_chan,
        (((1,), (1,)), ((), ())),
        preferred_element_type=jnp.float32,
    ).reshape(row_n, 9, -1)
    return jnp.einsum(
        "okc,lk->olc", chan_back, basis_tap.astype(jnp.float32), precision=lax.Precision.HIGHEST
    )


def on_device(
    acts_first,
    grads_first,
    acts_second,
    grads_second,
    grad_w,
    owner,
    basis_in,
    basis_spatial,
    basis_out,
):
    layer_inputs = ((acts_first, grads_first, 1), (acts_second, grads_second, 2))
    devices = lax.axis_size("dp") * lax.axis_size("group")
    channels = basis_in.shape[1]
    slot_total = basis_in.shape[0]
    row_count = grad_w.shape[1]
    row_start = lax.axis_index("dp") * row_count
    group_idx = lax.axis_index("group")
    layer_terms = [
        gram_terms(layer_inputs[idx][0], layer_inputs[idx][1], layer_inputs[idx][2])
        for idx in range(LAYERS)
    ]
    summed = []
    for layer_idx in range(LAYERS):
        summed.append(lax.psum(layer_terms[layer_idx], ("dp", "group")))
    full_grad = lax.all_gather(grad_w, "dp", axis=1, tiled=True)
    precond_list, fin_list, fsp_list, fout_list = ([], [], [], [])
    for layer_idx in range(LAYERS):
        images, grads_out, stride = layer_inputs[layer_idx]
        channel_s, spatial_s, output_s = summed[layer_idx]
        positions = images.shape[0] * grads_out.shape[1] * grads_out.shape[2] * devices
        channel_f = channel_s / (9.0 * positions)
        spatial_f = spatial_s / (1.0 * channels * positions)
        output_f = output_s / (1.0 * positions)
        flat_slot = owner[layer_idx]
        owner_group = flat_slot // slot_total
        local_slot = flat_slot % slot_total
        local_in = lax.dynamic_index_in_dim(basis_in, local_slot, 0, keepdims=False)
        local_tap = lax.dynamic_index_in_dim(basis_spatial, local_slot, 0, keepdims=False)
        local_out = lax.dynamic_index_in_dim(basis_out, local_slot, 0, keepdims=False)
        weights = full_grad[layer_idx].reshape(channels, 9, channels)

        def owner_rows():
            scale_in = eigen_values(local_in, channel_f)
            scale_tap = eigen_values(local_tap, spatial_f)
            scale_out = eigen_values(local_out, output_f)
            rotated = rotated_grad(weights, local_in, local_tap)
            coords = scaled_coords(rotated, local_out, scale_out, scale_tap, scale_in)
            rows_basis = lax.dynamic_slice_in_dim(local_out, row_start, row_count, 0)
            return (
                back_rows(coords, rows_basis, local_in, local_tap)
                .astype(jnp.bfloat16)
                .reshape(row_count, 9 * channels)
            )

        def empty_rows():
            return jnp.zeros((row_count, 9 * channels), jnp.bfloat16)

        own_rows = lax.cond(group_idx == owner_group, owner_rows, empty_rows)
        shared = from_root(own_rows, "group", owner_group)
        precond_list.append(shared)
        fin_list.append(channel_f)
        fsp_list.append(spatial_f)
        fout_list.append(output_f)
    return (jnp.stack(precond_list), jnp.stack(fin_list), jnp.stack(fsp_list), jnp.stack(fout_list))


def solution(mesh):
    placed = (
        P(("dp", "group"), None, None, None),
        P(("dp", "group"), None, None, None),
        P(("dp", "group"), None, None, None),
        P(("dp", "group"), None, None, None),
        P(None, "dp", None),
        P(),
        P("group", None, None),
        P("group", None, None),
        P("group", None, None),
    )
    return jax.shard_map(
        on_device,
        mesh=mesh,
        in_specs=placed,
        out_specs=(P(None, "dp", None), P(), P(), P()),
        check_vma=False,
    )
```

profile of v0, /device:TPU:0, one launch (start us, length us, event | category | flops | bytes accessed | tf_op | source)
XLA Modules:
  0.0 299.6 jit_solution(12308466518824444336)
XLA Ops:
  8.1 1.3 pad.8
  9.4 0.4 slice.80
  9.8 0.4 slice.81
  10.2 0.5 slice.82
  10.7 0.4 slice.83
  11.2 0.4 slice.84
  11.6 0.5 slice.85
  12.1 0.4 slice.86
  12.6 0.4 slice.87
  13.0 0.5 slice.88
  13.6 0.3 copy.401
  13.8 0.3 copy.402
  14.1 0.3 copy.403
  14.3 0.9 copy.404
  15.3 0.9 copy.405
  16.2 0.9 copy.406
  17.2 0.9 copy.407
  18.1 0.9 copy.408
  19.1 0.9 copy.409
  20.0 8.5 %stack.116 = bf16[9,1,16,16,256]{4,0,3,2,1:T(8,128)(2,1)S(1)} concatenate(bf16[1,1,16,16,256]{4,0,3,2,1:T(2,128)(2,1)S(1)} %copy.401, bf16[1,1,16,16,256]{4,0,3,2,1:T(2,128)(2,1)S(1)} %copy.402, bf16[1,1,16,16,256]{4,0,3,2,1:T(2,128)(2,1)S(1)} %copy.403, bf16[1,1,16,16,256]{4,0,3,2,1:T(2,128)(2,1)} %copy.404, bf16[1,1,16,16,256]{4,0,3,2,1:T(2,128)(2,1)} %copy.405, ...), dimensions={0} | concatenate | bytes 2359296 | tf_op jit(solution)/shard_map/stack | solution.py:33
  28.5 1.5 fusion.86
  30.0 0.7 fusion.102
  30.8 1.0 copy.387
  31.8 1.0 copy.388
  32.8 2.1 copy.389
  35.0 2.0 copy.390
  37.0 2.0 copy.392
  39.0 2.0 copy.393
  41.0 2.0 copy.394
  43.1 2.0 copy.395
  45.1 2.1 copy.391
  47.2 38.1 %stack.105 = bf16[9,1,32,32,256]{4,0,3,2,1:T(8,128)(2,1)} concatenate(bf16[1,1,32,32,256]{4,0,3,2,1:T(2,128)(2,1)S(1)} %copy.387, bf16[1,1,32,32,256]{4,0,3,2,1:T(2,128)(2,1)S(1)} %copy.388, bf16[1,1,32,32,256]{4,0,3,2,1:T(2,128)(2,1)} %copy.389, bf16[1,1,32,32,256]{4,0,3,2,1:T(2,128)(2,1)} %copy.390, bf16[1,1,32,32,256]{4,0,3,2,1:T(2,128)(2,1)} %copy.391, ...), dimensions={0} | concatenate | bytes 9437184 | tf_op jit(solution)/shard_map/stack | solution.py:33
  85.3 12.7 %fusion.89 = f32[256,256]{1,0:T(8,128)} fusion(bf16[9,32,32,256]{3,0,2,1:T(8,128)(2,1)} %bitcast.248), kind=kOutput, calls=%fused_computation.101 | convolution fusion | flops 1207959552 | bytes 4980736 | tf_op jit(solution)/shard_map/dot_general | solution.py:40
  98.0 1.0 convolution_bitcast_fusion.8
  99.0 0.9 convolution_bitcast_fusion.9
  100.0 0.8 copy.386
  100.9 0.6 fusion.112
  106.6 0.9 fusion.92
  107.5 9.4 %convolution_bitcast_fusion.10 = f32[9,9]{1,0:T(8,128)S(1)} fusion(bf16[9,1,32,32,256]{4,0,3,2,1:T(8,128)(2,1)} %stack.105), kind=kOutput, calls=%fused_computation.103 | convolution fusion | flops 42467328 | bytes 4718916 | tf_op jit(solution)/shard_map/dot_general | solution.py:44
  116.9 42.2 %all-reduce.2 = (f32[9,9]{1,0:T(8,128)S(1)}, f32[9,9]{1,0:T(8,128)S(1)}) all-reduce(f32[9,9]{1,0:T(8,128)S(1)} %fusion.92, f32[9,9]{1,0:T(8,128)S(1)} %convolution_bitcast_fusion.10), channel_id=1, replica_groups=mesh['dp'=16,'group'=2] {'dp','group'}, use_global_device_ids=true, to_apply=%region_10.11 | all-reduce | flops 162 | bytes 1296 | tf_op jit(solution)/shard_map/psum | solution.py:125
  159.1 0.6 copy.413
  159.8 82.6 %all-reduce.8.cloned.1.call-done = (f32[256,256]{1,0:T(8,128)}, f32[256,256]{1,0:T(8,128)}, f32[256,256]{1,0:T(8,128)}, f32[256,256]{1,0:T(8,128)}) async-done(((f32[256,256]{1,0:T(8,128)}, f32[256,256]{1,0:T(8,128)}, f32[256,256]{1,0:T(8,128)}, f32[256,256]{1,0:T(8,128)}), (f32[256,256]{1,0:T(8,128)}, f32[256,256]{1,0:T(8,128)}, f32[256,256]{1,0:T(8,128)}, ...) | async-done | bytes 1048592 | tf_op jit(solution)/shard_map/psum | solution.py:125
  242.3 2.0 fusion.108
  244.4 2.0 fusion.110
  246.4 25.6 %conditional.2 = (bf16[16,2304]{1,0:T(8,128)(2,1)S(1)}) conditional(s32[]{:T(128)} %convert_element_type.97, () %tuple.28, (s32[]{:T(128)}, s32[]{:T(128)}, bf16[4,256,256]{2,1,0:T(8,128)(2,1)}, bf16[4,256,256]{2,1,0:T(8,128)(2,1)S(1)}, bf16[2,256,2304]{2,0,1:T(2,128)(2,1)}, /*index=5*/bf16[4,9,9]{2,0,1:T(4,128)(2,1)S(1)}, ...), branch_computations={%region_3.4_spmd, %region_4.8_spmd.clone} | conditional | flops 1115490816 | bytes 36469280 | solution.py:159
  246.4 0.2 copy.433
  246.6 5.6 %copy.434 = bf16[2,256,2304]{1,2,0:T(8,128)(2,1)S(1)} copy(bf16[2,256,2304]{2,0,1:T(2,128)(2,1)} %get-tuple-element.537) | data formatting | bytes 4718592 | tf_op jit(solution)/shard_map
  252.3 0.5 convolution_bitcast_fusion
  252.8 3.4 %copy.430 = f32[256,9,256]{2,1,0:T(8,128)} copy(f32[256,9,256]{0,2,1:T(8,128)S(1)} %convolution_bitcast_fusion) | data formatting | bytes 4718592 | tf_op jit(solution)/shard_map/cond/branch_1_fun/dot_general | solution.py:61
  256.2 4.5 %convert_bitcast_fusion = bf16[256,9,256]{2,1,0:T(8,128)(2,1)S(1)} fusion(f32[256,9,256]{2,1,0:T(8,128)} %copy.430, bf16[4,9,9]{2,1,0:T(8,128)(2,1)S(1)} %copy.435, s32[]{:T(128)S(6)} %select_n.74), kind=kOutput, calls=%fused_computation.3 | convolution fusion | flops 64290816 | bytes 3543044 | tf_op jit(solution)/shard_map/cond/branch_1_fun/okj,kl->olj/dot_general | solution.py:64
  260.7 2.6 copy.431
  263.5 1.3 fusion.5
  264.8 0.2 mul.125
  265.0 2.0 copy.432
  267.0 1.4 fusion.6
  268.4 2.8 convolution_convert_fusion
  271.3 0.2 fusion.9
  271.5 0.3 convolution_convert_fusion.1
  272.0 0.6 select_bitcast_fusion.1
  272.7 0.6 select_bitcast_fusion
  273.3 1.9 pad_maximum_fusion.1
  275.2 1.9 pad_maximum_fusion
  277.0 13.5 %all-reduce.10.cloned.1.call-done = (bf16[1,16,2304]{2,1,0:T(8,128)(2,1)}, bf16[1,16,2304]{2,1,0:T(8,128)(2,1)}) async-done(((bf16[1,16,2304]{2,1,0:T(8,128)(2,1)}, bf16[1,16,2304]{2,1,0:T(8,128)(2,1)}), (bf16[1,16,2304]{2,1,0:T(8,128)(2,1)}, bf16[1,16,2304]{2,1,0:T(8,128)(2,1)})) %all-reduce.10.cloned.1.call-update) | async-done | bytes 147472 | tf_op jit(solution)/shard_map/psum | solution.py:14
  290.6 1.6 pad_maximum_fusion.2
  (41 shorter events, 0.6 us)
Async XLA Ops:
  8.0 90.0 %copy-start = (bf16[1,32,32,256]{3,2,1,0:T(8,128)(2,1)S(1)}, bf16[1,32,32,256]{3,2,1,0:T(8,128)(2,1)}, u32[]{:S(2)}) copy-start(bf16[1,32,32,256]{3,2,1,0:T(8,128)(2,1)} %param.14) | copy-start | bytes 1572868
  8.0 234.3 %all-reduce.8.cloned.1.call-start = ((), (), s32[]{:S(2)}) async-start(), calls=%async_computation.1 | async-start | bytes 2097152 | tf_op jit(solution)/shard_map/psum | solution.py:125
  28.5 1.5 copy-start.3
  28.5 1.5 copy-start.2
  98.0 1.1 copy-start.12
  99.0 1.0 copy-start.9
  99.0 1.9 copy-start.11
  99.0 7.5 %copy-start.4 = (bf16[9,1,16,16,256]{4,0,3,2,1:T(8,128)(2,1)S(1)}, bf16[9,1,16,16,256]{4,0,3,2,1:T(8,128)(2,1)}, u32[]{:S(2)}) copy-start(bf16[9,1,16,16,256]{4,0,3,2,1:T(8,128)(2,1)} %copy-done.3) | copy-start | bytes 3538948
  100.0 146.4 %all-gather.2.cloned.1.call-start = ((), (), s32[]{:S(2)}) async-start(), calls=%async_computation | async-start | bytes 2506752 | tf_op jit(solution)/shard_map/all_gather | solution.py:126
  100.8 189.7 %all-reduce.10.cloned.1.call-start = ((), (), s32[]{:S(2)}) async-start(), calls=%async_computation.2 | async-start | bytes 294912 | tf_op jit(solution)/shard_map/psum | solution.py:14
  116.9 129.5 %copy-start.5 = (bf16[4,256,256]{2,1,0:T(8,128)(2,1)S(1)}, bf16[4,256,256]{2,1,0:T(8,128)(2,1)}, u32[]{:S(2)}) copy-start(bf16[4,256,256]{2,1,0:T(8,128)(2,1)} %param.19) | copy-start | bytes 1572868
  116.9 129.5 %copy-start.10 = (bf16[4,9,9]{2,0,1:T(4,128)(2,1)S(1)}, bf16[4,9,9]{2,0,1:T(4,128)(2,1)}, u32[]{:S(2)}) copy-start(bf16[4,9,9]{2,0,1:T(4,128)(2,1)} %param.20) | copy-start | bytes 1948
  260.7 2.8 copy-start.8
  272.7 19.5 %copy-start.1 = (bf16[1,32,32,256]{3,2,1,0:T(8,128)(2,1)S(1)}, bf16[1,32,32,256]{3,2,1,0:T(8,128)(2,1)}, u32[]{:S(2)}) copy-start(bf16[1,32,32,256]{3,2,1,0:T(8,128)(2,1)} %param.14) | copy-start | bytes 1572868
Sparse Core Ops, SparseCore 0:
  100.1 142.1 all-reduce.7
  273.5 17.0 all-reduce.9
Sparse Core Ops, SparseCore 1:
  104.2 66.4 all-gather.1
where the time goes:
time: 305 us; the launch traced here: 300 us
  waiting for transfers between devices  96.1 us (32%)
  local copies, waits for them, and re-layouts  91.8 us (30%)
  blocking collectives  42.2 us (14%)
  matrix products  37.5 us (12%)
  between operations  20.7 us (7%)
  other arithmetic  10.8 us (4%)
    psum x1, waiting for transfers between devices, on_device(): summed.append(lax.psum(layer_terms[layer_idx], ('dp', 'group')))  82.6 us
    another operation x21, local copies, waits for them, and re-layouts, window_views(): return jnp.stack(windows)  70.2 us
    psum x1, blocking collectives, on_device(): summed.append(lax.psum(layer_terms[layer_idx], ('dp', 'group')))  42.2 us
    dot_general x2, matrix products, gram_terms(): lax.dot_general(patch_rows, patch_rows, (((0,), (0,)), ((), ())), preferr...  14.1 us
    psum x1, waiting for transfers between devices, from_root(): return lax.psum(block, axis)  13.5 us
    dot_general x2, matrix products, gram_terms(): lax.dot_general(tap_rows, tap_rows, (((1,), (1,)), ((), ())), preferred_e...  10.3 us
  transfers between devices with their start and end apart: 3, of which 2 were waited for; matrix products, arithmetic and copies ran while one was open for 7% of the time, Pallas kernels for 0%

commit v1 on v0

v1 whole, which is shorter than its diff:
```python
import functools

import jax
import jax.numpy as jnp
from jax import lax
from jax.experimental import pallas as pl
from jax.experimental.pallas import tpu as pltpu
from jax.sharding import PartitionSpec as P

LAYERS = 2
DAMPING = 0.1
LANES = 128
MESH = pl.DeviceIdType.MESH
F32 = jnp.float32
BF16 = jnp.bfloat16
HIGH = lax.Precision.HIGHEST
CONTRACT_ROWS = (((0,), (0,)), ((), ()))
CONTRACT_COLS = (((1,), (1,)), ((), ()))


def dot_rows(a, b, precision=None):
    return lax.dot_general(a, b, CONTRACT_ROWS, precision=precision, preferred_element_type=F32)


def dot_cols(a, b):
    return lax.dot_general(a, b, CONTRACT_COLS, preferred_element_type=F32)


def tap_count(idx, stride, out_side):
    total = jnp.zeros(idx.shape, jnp.int32)
    for off in range(3):
        base = idx + 1 - off
        hit = (base >= 0) & (base <= stride * (out_side - 1)) & (base % stride == 0)
        total = total + hit.astype(jnp.int32)
    return total


def channel_gram(x, side, stride, out_side):
    pos = lax.broadcasted_iota(jnp.int32, x.shape, 0)
    count = tap_count(pos // side, stride, out_side) * tap_count(pos % side, stride, out_side)
    total = None
    for digit in (1, 2, 4, 8):
        if digit > (9 if stride == 1 else 4):
            continue
        if stride == 1 and digit == 1:
            part = jnp.where((count & 1) != 0, x, jnp.zeros_like(x))
        else:
            part = jnp.where((count & digit) != 0, x * digit, jnp.zeros_like(x))
        term = dot_rows(part, x)
        total = term if total is None else total + term
    return total


def spatial_gram(xp_ref, v_ref, side, stride, out_side):
    total = None
    for i in range(out_side):
        rows = xp_ref[stride * i * side:(stride * i + 3) * side, :]
        term = dot_cols(rows, rows)
        total = term if total is None else total + term
    span = 3 * side
    left = lax.broadcasted_iota(jnp.int32, (span, span), 0) % side
    right = lax.broadcasted_iota(jnp.int32, (span, span), 1) % side
    v_ref[...] = jnp.zeros(v_ref.shape, F32)
    lane_in = lax.broadcasted_iota(jnp.int32, (LANES, LANES), 0)
    lane_out = lax.broadcasted_iota(jnp.int32, (LANES, LANES), 1)
    result = None
    for b2 in range(3):
        for b1 in range(3):
            base = left + 1 - b1
            mask = (right - left == b2 - b1) & (base >= 0) & (base <= stride * (out_side - 1))
            mask = mask & (base % stride == 0)
            kept = jnp.where(mask, total, 0.0)
            for a in range(3):
                t = 3 * a + b1
                v_ref[b2, t:t + 1, 0:span] = jnp.sum(
                    kept[a * side:(a + 1) * side], axis=0, keepdims=True)
        pick = ((lane_in < span) & (lane_out == 3 * (lane_in // side) + b2)).astype(F32)
        term = jnp.dot(v_ref[b2], pick, precision=HIGH, preferred_element_type=F32)
        result = term if result is None else result + term
    return result


def mixed_taps(parts, coef):
    out = []
    for t in range(9):
        total = parts[0] * coef(0, t)
        for u in range(1, 9):
            total = total + parts[u] * coef(u, t)
        out.append(total)
    return out


def through_basis(parts, basis, rows, flip):
    def product(a):
        if flip:
            return dot_cols(a, basis)
        return jnp.dot(a, basis, preferred_element_type=F32)
    if rows % 16 == 0:
        whole = product(jnp.concatenate(parts, axis=0))
        return [whole[u * rows:(u + 1) * rows] for u in range(9)]
    return [product(part) for part in parts]


def local_kernel(dims, info_ref, qs_ref, x0_ref, g0_ref, x1_ref, g1_ref, w_ref, qa_ref,
                 gram_ref, rot_ref, xp_ref, v_ref):
    side, outs, strides, images, chans, rows, dp = dims
    for l, (x_ref, g_ref) in enumerate(((x0_ref, g0_ref), (x1_ref, g1_ref))):
        base = l * 2 * chans
        fin = fsp = None
        xp_ref[0:side, :] = jnp.zeros((side, chans), BF16)
        xp_ref[side * (side + 1):side * (side + 2), :] = jnp.zeros((side, chans), BF16)
        for n in range(images):
            x = x_ref[n * side * side:(n + 1) * side * side, :]
            xp_ref[side:side * (side + 1), :] = x
            part = channel_gram(x, side, strides[l], outs[l])
            fin = part if fin is None else fin + part
            part = spatial_gram(xp_ref, v_ref, side, strides[l], outs[l])
            fsp = part if fsp is None else fsp + part
        g = g_ref[...]
        gram_ref[base:base + chans, :] = fin.astype(BF16)
        half = chans // 2
        gram_ref[base + half:base + half + 16, 0:LANES] = fsp.astype(BF16)
        gram_ref[base + chans:base + 2 * chans, :] = dot_rows(g, g).astype(BF16)
    per = 9 * chans // LANES
    for k in range(LAYERS * per, rot_ref.shape[0] * rot_ref.shape[1]):
        rot_ref[k % dp, k // dp] = jnp.zeros((rows, LANES), BF16)
    for l in range(LAYERS):
        basis = qa_ref[info_ref[l]]
        parts = [w_ref[l, :, u * chans:(u + 1) * chans] for u in range(9)]
        inner = through_basis(parts, basis, rows, False)
        turned = mixed_taps(inner, lambda u, t: qs_ref[l, 9 * u + t])
        for c in range(per):
            k = l * per + c
            lane = (c * LANES) % chans
            rot_ref[k % dp, k // dp] = turned[c * LANES // chans][:, lane:lane + LANES].astype(BF16)


def remote(src, dst, send, recv, axis, peer):
    return pltpu.make_async_remote_copy(src_ref=src, dst_ref=dst, send_sem=send, recv_sem=recv,
                                        device_id={axis: peer}, device_id_type=MESH)


def enter(dp, ng, me, grp):
    barrier = pltpu.get_barrier_semaphore()

    def greet(k, c):
        pl.semaphore_signal(barrier, inc=1, device_id={"dp": lax.rem(me + k, dp)},
                            device_id_type=MESH)
        return c
    lax.fori_loop(1, dp, greet, 0)
    for q in range(1, ng):
        pl.semaphore_signal(barrier, inc=1, device_id={"group": lax.rem(grp + q, ng)},
                            device_id_type=MESH)
    pl.semaphore_wait(barrier, dp + ng - 2)


def each(n, fn):
    def body(k, c):
        fn(k)
        return c
    lax.fori_loop(1, n, body, 0)


def share_kernel(dp, ng, gram_ref, rot_ref, full_ref, rotin_ref, ga_ref, h_ref, hb_ref,
                 sa, ra, sb, rb, sc, rc, sd, rd, st, rt, lt):
    me, grp = lax.axis_index("dp"), lax.axis_index("group")
    enter(dp, ng, me, grp)

    def copy_a(q):
        to = lax.rem(grp + q, ng)
        return remote(gram_ref.at[to], ga_ref.at[q - 1], sa.at[q], ra.at[q], "group", to)

    def copy_t(k):
        to = lax.rem(me + k, dp)
        return remote(rot_ref.at[to], rotin_ref.at[:, me], st.at[k], rt.at[k], "dp", to)

    def copy_b(k):
        to = lax.rem(me + k, dp)
        return remote(h_ref.at[to], hb_ref.at[k - 1], sb.at[k], rb.at[k], "dp", to)

    def copy_c(k):
        to = lax.rem(me + k, dp)
        return remote(full_ref.at[grp, me], full_ref.at[grp, me], sc.at[k], rc.at[k], "dp", to)

    def copy_d(k, q):
        to = lax.rem(grp + q, ng)
        block = full_ref.at[grp, lax.rem(me + dp - k, dp)]
        return remote(block, block, sd.at[q, k], rd.at[q, k], "group", to)

    own = pltpu.make_async_copy(rot_ref.at[me], rotin_ref.at[:, me], lt)
    for q in range(1, ng):
        copy_a(q).start()
    own.start()
    each(dp, lambda k: copy_t(k).start())
    for q in range(1, ng):
        copy_a(q).wait_recv()
    total = gram_ref[grp].astype(F32)
    for q in range(1, ng):
        total = total + ga_ref[q - 1].astype(F32)
    h_ref[...] = total.astype(BF16)
    each(dp, lambda k: copy_b(k).start())
    each(dp, lambda k: copy_b(k).wait_recv())
    total = h_ref[me].astype(F32)
    total = lax.fori_loop(0, dp - 1, lambda k, t: t + hb_ref[k].astype(F32), total)
    full_ref[grp, me] = total.astype(BF16)
    each(dp, lambda k: copy_c(k).start())
    for q in range(1, ng):
        copy_d(0, q).start()

    def pass_on(k):
        copy_c(k).wait_recv()
        for q in range(1, ng):
            copy_d(k, q).start()
    each(dp, pass_on)
    for q in range(1, ng):
        copy_d(0, q).wait()
    for q in range(1, ng):
        copy_a(q).wait_send()

    def finish(k):
        copy_b(k).wait_send()
        copy_c(k).wait_send()
        copy_t(k).wait()
        for q in range(1, ng):
            copy_d(k, q).wait()
    each(dp, finish)
    own.wait()


def coords_kernel(dims, info_ref, gram_ref, rot_ref, qa_ref, qg_ref, qs_ref,
                  back_ref, fin_ref, fsp_ref, fout_ref, lin_ref, ltap_ref, lout_ref):
    chans, dp, slots, positions = dims
    half = chans // 2
    for l in range(LAYERS):
        base = l * 2 * chans
        fin = gram_ref[base:base + chans, :]
        corner = jnp.transpose(fin[0:half, half:chans].astype(F32))
        low = jnp.concatenate([corner, fin[half:chans, half:chans].astype(F32)], axis=1)
        fin = jnp.concatenate([fin[0:half].astype(F32), low], axis=0)
        fsp = gram_ref[base + half:base + half + 16, 0:LANES].astype(F32)
        fout = gram_ref[base + chans:base + 2 * chans, :]
        fsp = fsp / (1.0 * chans * positions[l])
        fin_ref[l] = fin / (9.0 * positions[l])
        fout_ref[l] = fout.astype(F32) / (1.0 * positions[l])
        fsp_ref[l] = fsp[0:9, 0:9]
        qa, qg, qs = qa_ref[info_ref[l]], qg_ref[info_ref[l]], qs_ref[l]
        prod = jnp.dot(fin.astype(BF16), qa, preferred_element_type=F32)
        lin_ref[l] = jnp.sum(qa.astype(F32) * prod, axis=0, keepdims=True) / (9.0 * positions[l])
        prod = qg.astype(F32) * jnp.dot(fout, qg, preferred_element_type=F32)
        lout_ref[l] = dot_rows(prod / (1.0 * positions[l]), jnp.ones((chans, LANES), F32), HIGH)
        turned = fsp[:, 0:1] * qs[0:1, :]
        for v in range(1, 9):
            turned = turned + fsp[:, v:v + 1] * qs[v:v + 1, :]
        ltap_ref[l] = jnp.sum(turned * qs, axis=0, keepdims=True)
    per = 9 * chans // LANES
    split = chans // LANES
    for s in range(slots):
        k = jnp.minimum(s * dp + info_ref[4], LAYERS * per - 1)
        l = k // per
        c = k % per
        lane = lax.broadcasted_iota(jnp.int32, (1, LANES), 1)
        tap = jnp.sum(jnp.where(lane == c // split, ltap_ref[l], 0.0), axis=1, keepdims=True)
        row = lin_ref[l]
        scale_in = row[:, 0:LANES]
        for piece in range(1, split):
            scale_in = jnp.where(c % split == piece, row[:, piece * LANES:(piece + 1) * LANES],
                                 scale_in)
        qg = qg_ref[info_ref[l]]
        projected = dot_rows(qg, rot_ref[s])
        divisor = (lout_ref[l] * tap) * scale_in + DAMPING
        coords = (projected / divisor).astype(BF16)
        back_ref[s] = jnp.dot(qg, coords, preferred_element_type=F32).astype(BF16)


def rows_kernel(dims, info_ref, qs_ref, back_ref, qa_ref, out_ref, in_ref, own_ref, peer_ref,
                st, rt, lt, sx, rx):
    dp, ng, rows, chans = dims
    me, grp = lax.axis_index("dp"), lax.axis_index("group")
    enter(dp, ng, me, grp)

    def copy_t(k):
        to = lax.rem(me + k, dp)
        return remote(back_ref.at[:, to], in_ref.at[me], st.at[k], rt.at[k], "dp", to)

    def copy_x(q):
        return remote(own_ref, peer_ref.at[q - 1], sx.at[q], rx.at[q], "group",
                      lax.rem(grp + q, ng))

    own = pltpu.make_async_copy(back_ref.at[:, me], in_ref.at[me], lt)
    own.start()
    each(dp, lambda k: copy_t(k).start())
    own.wait()
    each(dp, lambda k: copy_t(k).wait())
    per = 9 * chans // LANES
    split = chans // LANES
    for l in range(LAYERS):
        basis = qa_ref[info_ref[l]]
        mine = info_ref[2 + l] == 1
        parts = []
        for t in range(9):
            pieces = []
            for piece in range(split):
                k = l * per + t * split + piece
                pieces.append(in_ref[k % dp, k // dp])
            parts.append(jnp.concatenate(pieces, axis=1))
        chan = through_basis(parts, basis, rows, True)
        turned = mixed_taps(chan, lambda t, u: qs_ref[l, 9 * u + t])
        for u in range(9):
            value = jnp.where(mine, turned[u], jnp.zeros_like(turned[u]))
            own_ref[l, :, u * chans:(u + 1) * chans] = value.astype(BF16)
    for q in range(1, ng):
        copy_x(q).start()
    for q in range(1, ng):
        copy_x(q).wait()
    total = own_ref[...]
    for q in range(1, ng):
        total = total + peer_ref[q - 1]
    out_ref[...] = total


def on_device(dp, ng, acts_first, grads_first, acts_second, grads_second, grad_w, owner,
              basis_in, basis_spatial, basis_out):
    images, side = acts_first.shape[0], acts_first.shape[1]
    chans = basis_in.shape[1]
    rows = grad_w.shape[1]
    slot_total = basis_in.shape[0]
    outs = (grads_first.shape[1], grads_second.shape[1])
    positions = tuple(images * o * o * dp * ng for o in outs)
    slots = -(-LAYERS * 9 * chans // LANES // dp)
    gram_rows = 2 * LAYERS * chans
    slice_rows = gram_rows // (dp * ng)
    vmem = pl.BlockSpec(memory_space=pltpu.VMEM)
    smem = pl.BlockSpec(memory_space=pltpu.SMEM)
    struct = jax.ShapeDtypeStruct
    dma = pltpu.SemaphoreType.DMA

    local = owner % slot_total
    holds = (owner // slot_total == lax.axis_index("group")).astype(jnp.int32)
    info = jnp.concatenate([local, holds, lax.axis_index("dp").astype(jnp.int32)[None]])
    taps = jnp.stack([lax.dynamic_index_in_dim(basis_spatial, local[l], 0, keepdims=False)
                      for l in range(LAYERS)]).astype(F32)
    taps_flat = taps.reshape(LAYERS, 81)
    taps_wide = jnp.pad(taps, ((0, 0), (0, 7), (0, LANES - 9)))

    gram, rot = pl.pallas_call(
        functools.partial(local_kernel, (side, outs, (1, 2), images, chans, rows, dp)),
        out_shape=(struct((gram_rows, chans), BF16), struct((dp, slots, rows, LANES), BF16)),
        in_specs=[smem, smem] + [vmem] * 6,
        out_specs=(vmem, vmem),
        scratch_shapes=[pltpu.VMEM(((side + 2) * side, chans), BF16),
                        pltpu.VMEM((3, 16, LANES), F32)],
        compiler_params=pltpu.CompilerParams(vmem_limit_bytes=40 << 20),
        name="local_terms",
    )(info, taps_flat, acts_first.reshape(-1, chans), grads_first.reshape(-1, chans),
      acts_second.reshape(-1, chans), grads_second.reshape(-1, chans), grad_w, basis_in)

    full, rotin = pl.pallas_call(
        functools.partial(share_kernel, dp, ng),
        out_shape=(struct((ng, dp, slice_rows, chans), BF16),
                   struct((slots, dp, rows, LANES), BF16)),
        in_specs=[vmem, vmem],
        out_specs=(vmem, vmem),
        scratch_shapes=[pltpu.VMEM((ng - 1, dp, slice_rows, chans), BF16),
                        pltpu.VMEM((dp, slice_rows, chans), BF16),
                        pltpu.VMEM((dp - 1, slice_rows, chans), BF16),
                        dma((ng,)), dma((ng,)), dma((dp,)), dma((dp,)), dma((dp,)), dma((dp,)),
                        dma((ng, dp)), dma((ng, dp)), dma((dp,)), dma((dp,)), dma],
        compiler_params=pltpu.CompilerParams(collective_id=0, has_side_effects=True,
                                             vmem_limit_bytes=32 << 20),
        name="share_sums",
    )(gram.reshape(ng, dp, slice_rows, chans), rot)

    back, fin, fsp, fout = pl.pallas_call(
        functools.partial(coords_kernel, (chans, dp, slots, positions)),
        out_shape=(struct((slots, chans, LANES), BF16), struct((LAYERS, chans, chans), F32),
                   struct((LAYERS, 9, 9), F32), struct((LAYERS, chans, chans), F32)),
        in_specs=[smem] + [vmem] * 5,
        out_specs=(vmem,) * 4,
        scratch_shapes=[pltpu.VMEM((LAYERS, 1, chans), F32), pltpu.VMEM((LAYERS, 1, LANES), F32),
                        pltpu.VMEM((LAYERS, chans, LANES), F32)],
        compiler_params=pltpu.CompilerParams(vmem_limit_bytes=32 << 20),
        name="scaled_coords",
    )(info, full.reshape(gram_rows, chans), rotin.reshape(slots, chans, LANES),
      basis_in, basis_out, taps_wide)

    precond = pl.pallas_call(
        functools.partial(rows_kernel, (dp, ng, rows, chans)),
        out_shape=struct((LAYERS, rows, 9 * chans), BF16),
        in_specs=[smem, smem, vmem, vmem],
        out_specs=vmem,
        scratch_shapes=[pltpu.VMEM((dp, slots, rows, LANES), BF16),
                        pltpu.VMEM((LAYERS, rows, 9 * chans), BF16),
                        pltpu.VMEM((ng - 1, LAYERS, rows, 9 * chans), BF16),
                        dma((dp,)), dma((dp,)), dma, dma((ng,)), dma((ng,))],
        compiler_params=pltpu.CompilerParams(collective_id=1, has_side_effects=True,
                                             vmem_limit_bytes=32 << 20),
        name="back_rows",
    )(info, taps_flat, back.reshape(slots, dp, rows, LANES), basis_in)
    return precond, fin, fsp, fout


def solution(mesh):
    placed = (
        P(("dp", "group"), None, None, None),
        P(("dp", "group"), None, None, None),
        P(("dp", "group"), None, None, None),
        P(("dp", "group"), None, None, None),
        P(None, "dp", None),
        P(),
        P("group", None, None),
        P("group", None, None),
        P("group", None, None),
    )
    return jax.shard_map(
        functools.partial(on_device, mesh.shape["dp"], mesh.shape["group"]),
        mesh=mesh,
        in_specs=placed,
        out_specs=(P(None, "dp", None), P(), P(), P()),
        check_vma=False,
    )
```

time: 305 us -> 60.1 us (0.20); the launches traced: 300 us -> 59.6 us
  waiting for transfers between devices: 96.1 us -> 0 us
  local copies, waits for them, and re-layouts: 91.8 us -> 8.68 us
  Pallas kernels: 0 us -> 46.2 us
  blocking collectives: 42.2 us -> 0 us
  matrix products: 37.5 us -> 0 us
  between operations: 20.7 us -> 4.64 us
  other arithmetic: 10.8 us -> 0.12 us
    psum x2 -> x0, waiting for transfers between devices: 96.1 us -> none  [the longest x1 82.6 us: on_device(): summed.append(lax.psum(layer_terms[layer_idx], ('dp', 'group')))]
    another operation x25 -> x2, local copies, waits for them, and re-layouts: 76 us -> 0.18 us  [on_device(): jnp.stack([lax.dynamic_index_in_dim(basis_spatial, local[l], 0, keepdims=...]
    pallas_call x0 -> x4, Pallas kernels: none -> 46.2 us  [the longest x1 27.6 us: on_device(): pl.pallas_call(functools.partial(share_kernel, dp, ng), out_shape=(struct...]
    psum x1 -> x0, blocking collectives: 42.2 us -> none  [on_device(): summed.append(lax.psum(layer_terms[layer_idx], ('dp', 'group')))]
    dot_general x14 -> x0, matrix products: 37.5 us -> none  [the longest x2 14.1 us: gram_terms(): lax.dot_general(patch_rows, patch_rows, (((0,), (0,)), ((), ())), preferr...]
    another operation x9 -> x0, other arithmetic: 10.7 us -> none  [the longest x3 5.94 us: on_device(): jnp.stack(fout_list)]
    unnamed x22, local copies, waits for them, and re-layouts: 1.43 us -> 7.9 us
    slice x11 -> x1, local copies, waits for them, and re-layouts: 4.77 us -> 0.58 us  [on_device(): local[l]]
  transfers between devices with their start and end apart: 3 -> 0, of which waited for: 2 -> 0; matrix products, arithmetic and copies ran while one was open for 7% -> 0% of each run, Pallas kernels for 0% -> 0%
where the time goes in v1:
time: 60.1 us; the launch traced here: 59.6 us
  Pallas kernels  46.2 us (77%)
  local copies, waits for them, and re-layouts  8.68 us (14%)
  between operations  4.64 us (8%)
    pallas_call x1, Pallas kernels, on_device(): pl.pallas_call(functools.partial(share_kernel, dp, ng), out_shape=(struct...  27.6 us
    pallas_call x1, Pallas kernels, on_device(): pl.pallas_call(functools.partial(rows_kernel, (dp, ng, rows, chans)), out...  11.9 us
    unnamed x22, local copies, waits for them, and re-layouts  7.9 us
    pallas_call x1, Pallas kernels, on_device(): pl.pallas_call(functools.partial(local_kernel, (side, outs, (1, 2), image...  4.25 us
    pallas_call x1, Pallas kernels, on_device(): pl.pallas_call(functools.partial(coords_kernel, (chans, dp, slots, positi...  2.5 us

profile of v1, /device:TPU:0, one launch (start us, length us, event | category | flops | bytes accessed | tf_op | source)
XLA Modules:
  0.0 59.6 jit_solution(13981332793055306812)
XLA Ops:
  0.6 0.0 copy-start.8
  0.6 0.6 %copy-done.8 = s32[2]{0:T(128)S(1)} copy-done((s32[2]{0:T(128)S(1)}, s32[2]{0:T(128)}, u32[]{:S(2)}) %copy-start.8) | copy-done | bytes 32
  1.3 0.1 pad_add_fusion.info_ref
  1.4 0.6 fusion.7
  2.0 0.0 copy-start.7
  5.9 0.0 copy-done.7
  5.9 0.1 stack.11
  6.0 0.1 stack.12
  6.1 0.0 copy-start
  6.1 1.0 %copy-done = bf16[4,256,256]{2,1,0:T(8,128)(2,1)S(1)} copy-done((bf16[4,256,256]{2,1,0:T(8,128)(2,1)S(1)}, bf16[4,256,256]{2,1,0:T(8,128)(2,1)}, u32[]{:S(2)}) %copy-start) | copy-done | bytes 524312
  7.2 0.0 copy-start.1
  7.2 1.0 %copy-done.1 = bf16[1,32,32,256]{3,2,1,0:T(8,128)(2,1)S(1)} copy-done((bf16[1,32,32,256]{3,2,1,0:T(8,128)(2,1)S(1)}, bf16[1,32,32,256]{3,2,1,0:T(8,128)(2,1)}, u32[]{:S(2)}) %copy-start.1) | copy-done | bytes 524312
  8.2 0.0 copy-start.2
  8.2 1.0 %copy-done.2 = bf16[1,32,32,256]{3,2,1,0:T(8,128)(2,1)S(1)} copy-done((bf16[1,32,32,256]{3,2,1,0:T(8,128)(2,1)S(1)}, bf16[1,32,32,256]{3,2,1,0:T(8,128)(2,1)}, u32[]{:S(2)}) %copy-start.2) | copy-done | bytes 524312
  9.3 0.0 copy-start.3
  9.3 1.0 %copy-done.3 = bf16[1,32,32,256]{3,2,1,0:T(8,128)(2,1)S(1)} copy-done((bf16[1,32,32,256]{3,2,1,0:T(8,128)(2,1)S(1)}, bf16[1,32,32,256]{3,2,1,0:T(8,128)(2,1)}, u32[]{:S(2)}) %copy-start.3) | copy-done | bytes 524312
  10.3 0.0 copy-start.5
  10.3 0.9 %copy-done.5 = bf16[2,16,2304]{2,1,0:T(8,128)(2,1)S(1)} copy-done((bf16[2,16,2304]{2,1,0:T(8,128)(2,1)S(1)}, bf16[2,16,2304]{2,1,0:T(8,128)(2,1)}, u32[]{:S(2)}) %copy-start.5) | copy-done | bytes 147480
  11.2 0.0 copy-start.6
  11.2 0.9 %copy-done.6 = bf16[1,16,16,256]{3,2,1,0:T(8,128)(2,1)S(1)} copy-done((bf16[1,16,16,256]{3,2,1,0:T(8,128)(2,1)S(1)}, bf16[1,16,16,256]{3,2,1,0:T(8,128)(2,1)}, u32[]{:S(2)}) %copy-start.6) | copy-done | bytes 131096
  12.1 4.3 %local_terms.1 = (bf16[1024,256]{1,0:T(8,128)(2,1)S(1)}, bf16[16,3,16,128]{3,2,1,0:T(8,128)(2,1)S(1)}) custom-call(s32[5]{0:T(128)S(1)} %pad_add_fusion.info_ref, f32[2,81]{1,0:T(2,128)S(1)} %maximum_convert_fusion.qs_ref, bf16[1024,256]{1,0:T(8,128)(2,1)S(1)} %bitcast.11, bf16[1024,256]{1,0:T(8,128)(2,1)S(1)} %bitcast.12, bf16[1024,256]{1,0:T(8,128)(2,1)S(1)} %bitcast.13, ...), custom_call_target="tpu_custom_call" | custom-call | tf_op jit(solution)/shard_map/local_terms/pallas_call | solution.py:345
  16.4 0.0 copy-start.4
  16.4 27.6 %share_sums.1 = (bf16[2,16,32,256]{3,2,1,0:T(8,128)(2,1)S(1)}, bf16[3,16,16,128]{3,2,1,0:T(8,128)(2,1)S(1)}) custom-call(bf16[2,16,32,256]{3,2,1,0:T(8,128)(2,1)S(1)} %bitcast.14, bf16[16,3,16,128]{3,2,1,0:T(8,128)(2,1)S(1)} %get-tuple-element.13.rot_ref), custom_call_target="tpu_custom_call" | custom-call | tf_op jit(solution)/shard_map/share_sums/pallas_call | solution.py:357
  44.0 0.0 copy-done.4
  44.0 2.5 %scaled_coords.1 = (bf16[3,256,128]{2,1,0:T(8,128)(2,1)S(1)}, f32[2,256,256]{2,1,0:T(8,128)}, f32[2,9,9]{2,1,0:T(8,128)S(1)}, f32[2,256,256]{2,1,0:T(8,128)}) custom-call(s32[5]{0:T(128)S(1)} %pad_add_fusion.info_ref, bf16[1024,256]{1,0:T(8,128)(2,1)S(1)} %bitcast.15, bf16[3,256,128]{2,1,0:T(8,128)(2,1)S(1)} %bitcast.17, bf16[4,256,256]{2,1,0:T(8,128)(2,1)S(1)} %copy-done, ...), custom_call_target="tpu_custom_call" | custom-call | tf_op jit(solution)/shard_map/scaled_coords/pallas_call | solution.py:373
  46.5 11.9 %back_rows.1 = bf16[2,16,2304]{2,1,0:T(8,128)(2,1)S(1)} custom-call(s32[5]{0:T(128)S(1)} %pad_add_fusion.info_ref, f32[2,81]{1,0:T(2,128)S(1)} %maximum_convert_fusion.qs_ref, bf16[3,16,16,128]{3,2,1,0:T(8,128)(2,1)S(1)} %bitcast.16, bf16[4,256,256]{2,1,0:T(8,128)(2,1)S(1)} %copy-done), custom_call_target="tpu_custom_call" | custom-call | tf_op jit(solution)/shard_map/back_rows/pallas_call | solution.py:386
  58.4 0.6 %copy.15 = f32[2,9,9]{2,0,1:T(2,128)} copy(f32[2,9,9]{2,1,0:T(8,128)S(1)} %get-tuple-element.22) | data formatting | bytes 1296
  59.0 0.7 %copy.19 = bf16[2,16,2304]{2,1,0:T(8,128)(2,1)} copy(bf16[2,16,2304]{2,1,0:T(8,128)(2,1)S(1)} %back_rows.1) | data formatting | bytes 294912
  (7 shorter events, 0.1 us)
Async XLA Ops:
  0.6 0.7 %copy-start.8 = (s32[2]{0:T(128)S(1)}, s32[2]{0:T(128)}, u32[]{:S(2)}) copy-start(s32[2]{0:T(128)} %param.14) | copy-start | bytes 28
  2.0 3.9 %copy-start.7 = (bf16[4,9,9]{2,0,1:T(4,128)(2,1)S(1)}, bf16[4,9,9]{2,0,1:T(4,128)(2,1)}, u32[]{:S(2)}) copy-start(bf16[4,9,9]{2,0,1:T(4,128)(2,1)} %param.16) | copy-start | bytes 1948
  6.1 1.0 %copy-start = (bf16[4,256,256]{2,1,0:T(8,128)(2,1)S(1)}, bf16[4,256,256]{2,1,0:T(8,128)(2,1)}, u32[]{:S(2)}) copy-start(bf16[4,256,256]{2,1,0:T(8,128)(2,1)} %qa_ref.5) | copy-start | bytes 1572868
  7.2 1.0 %copy-start.1 = (bf16[1,32,32,256]{3,2,1,0:T(8,128)(2,1)S(1)}, bf16[1,32,32,256]{3,2,1,0:T(8,128)(2,1)}, u32[]{:S(2)}) copy-start(bf16[1,32,32,256]{3,2,1,0:T(8,128)(2,1)} %param.9) | copy-start | bytes 1572868
  8.2 1.0 %copy-start.2 = (bf16[1,32,32,256]{3,2,1,0:T(8,128)(2,1)S(1)}, bf16[1,32,32,256]{3,2,1,0:T(8,128)(2,1)}, u32[]{:S(2)}) copy-start(bf16[1,32,32,256]{3,2,1,0:T(8,128)(2,1)} %param.10) | copy-start | bytes 1572868
  9.3 1.0 %copy-start.3 = (bf16[1,32,32,256]{3,2,1,0:T(8,128)(2,1)S(1)}, bf16[1,32,32,256]{3,2,1,0:T(8,128)(2,1)}, u32[]{:S(2)}) copy-start(bf16[1,32,32,256]{3,2,1,0:T(8,128)(2,1)} %param.11) | copy-start | bytes 1572868
  10.3 0.9 %copy-start.5 = (bf16[2,16,2304]{2,1,0:T(8,128)(2,1)S(1)}, bf16[2,16,2304]{2,1,0:T(8,128)(2,1)}, u32[]{:S(2)}) copy-start(bf16[2,16,2304]{2,1,0:T(8,128)(2,1)} %w_ref.1) | copy-start | bytes 442372
  11.2 0.9 %copy-start.6 = (bf16[1,16,16,256]{3,2,1,0:T(8,128)(2,1)S(1)}, bf16[1,16,16,256]{3,2,1,0:T(8,128)(2,1)}, u32[]{:S(2)}) copy-start(bf16[1,16,16,256]{3,2,1,0:T(8,128)(2,1)} %param.12) | copy-start | bytes 393220
  16.4 27.6 %copy-start.4 = (bf16[4,256,256]{2,1,0:T(8,128)(2,1)S(1)}, bf16[4,256,256]{2,1,0:T(8,128)(2,1)}, u32[]{:S(2)}) copy-start(bf16[4,256,256]{2,1,0:T(8,128)(2,1)} %qg_ref.1) | copy-start | bytes 1572868

commit v2 on v1

--- a/solution.py
+++ b/solution.py
@@ -101,12 +101,38 @@
     return [product(part) for part in parts]
 
 
-def local_kernel(dims, info_ref, qs_ref, x0_ref, g0_ref, x1_ref, g1_ref, w_ref, qa_ref,
-                 gram_ref, rot_ref, xp_ref, v_ref):
-    side, outs, strides, images, chans, rows, dp = dims
+def put_rows(ref, dp, start, value):
+    size = ref.shape[2]
+    step = min(size, value.shape[0])
+    for j in range(0, value.shape[0], step):
+        i, off = divmod(start + j, size)
+        piece = value[j:j + step].astype(BF16)
+        ref[i // dp, i % dp, off:off + step, 0:value.shape[1]] = piece
+
+
+def local_loads(pairs, sems):
+    loads = {}
+    for i, (src, dst) in enumerate(pairs):
+        step = dst.shape[0] // 4 if dst.shape[0] % 4 == 0 else dst.shape[0] // 2
+        loads[i] = [pltpu.make_async_copy(src.at[pl.ds(j * step, step)],
+                                          dst.at[pl.ds(j * step, step)], sems.at[i, j])
+                    for j in range(dst.shape[0] // step)]
+    for i in range(len(pairs)):
+        for load in loads[i]:
+            load.start()
+
+    def arrive(i):
+        for load in loads[i]:
+            load.wait()
+    return arrive
+
+
+def local_grams(dims, arrive, x0_ref, g0_ref, x1_ref, g1_ref, gram_ref, xp_ref, v_ref):
+    side, outs, strides, images, chans, rows, dp, slot_total = dims
     for l, (x_ref, g_ref) in enumerate(((x0_ref, g0_ref), (x1_ref, g1_ref))):
         base = l * 2 * chans
         fin = fsp = None
+        arrive(2 * l)
         xp_ref[0:side, :] = jnp.zeros((side, chans), BF16)
         xp_ref[side * (side + 1):side * (side + 2), :] = jnp.zeros((side, chans), BF16)
         for n in range(images):
@@ -116,19 +142,25 @@
             fin = part if fin is None else fin + part
             part = spatial_gram(xp_ref, v_ref, side, strides[l], outs[l])
             fsp = part if fsp is None else fsp + part
+        arrive(2 * l + 1)
         g = g_ref[...]
-        gram_ref[base:base + chans, :] = fin.astype(BF16)
+        put_rows(gram_ref, dp, base, fin)
         half = chans // 2
-        gram_ref[base + half:base + half + 16, 0:LANES] = fsp.astype(BF16)
-        gram_ref[base + chans:base + 2 * chans, :] = dot_rows(g, g).astype(BF16)
+        put_rows(gram_ref, dp, base + half, fsp)
+        put_rows(gram_ref, dp, base + chans, dot_rows(g, g))
+
+
+def local_rotation(dims, owner_ref, qs_ref, w_ref, qa_ref, rot_ref):
+    side, outs, strides, images, chans, rows, dp, slot_total = dims
+    slots = [owner_ref[l] % slot_total for l in range(LAYERS)]
     per = 9 * chans // LANES
     for k in range(LAYERS * per, rot_ref.shape[0] * rot_ref.shape[1]):
         rot_ref[k % dp, k // dp] = jnp.zeros((rows, LANES), BF16)
     for l in range(LAYERS):
-        basis = qa_ref[info_ref[l]]
+        basis = qa_ref[slots[l]]
         parts = [w_ref[l, :, u * chans:(u + 1) * chans] for u in range(9)]
         inner = through_basis(parts, basis, rows, False)
-        turned = mixed_taps(inner, lambda u, t: qs_ref[l, 9 * u + t])
+        turned = mixed_taps(inner, lambda u, t: qs_ref[slots[l], 9 * u + t])
         for c in range(per):
             k = l * per + c
             lane = (c * LANES) % chans
@@ -140,7 +172,7 @@
                                         device_id={axis: peer}, device_id_type=MESH)
 
 
-def enter(dp, ng, me, grp):
+def greet_all(dp, ng, me, grp):
     barrier = pltpu.get_barrier_semaphore()
 
     def greet(k, c):
@@ -151,7 +183,15 @@
     for q in range(1, ng):
         pl.semaphore_signal(barrier, inc=1, device_id={"group": lax.rem(grp + q, ng)},
                             device_id_type=MESH)
-    pl.semaphore_wait(barrier, dp + ng - 2)
+
+
+def all_here(dp, ng):
+    pl.semaphore_wait(pltpu.get_barrier_semaphore(), dp + ng - 2)
+
+
+def enter(dp, ng, me, grp):
+    greet_all(dp, ng, me, grp)
+    all_here(dp, ng)
 
 
 def each(n, fn):
@@ -161,10 +201,17 @@
     lax.fori_loop(1, n, body, 0)
 
 
-def share_kernel(dp, ng, gram_ref, rot_ref, full_ref, rotin_ref, ga_ref, h_ref, hb_ref,
+def share_kernel(dims, ng, owner_ref, qs_ref, x0_hbm, g0_hbm, x1_hbm, g1_hbm, w_hbm, qa_hbm,
+                 full_ref, rotin_ref, gram_ref, rot_ref, x0_ref, g0_ref, x1_ref, g1_ref, w_ref,
+                 qa_ref, xp_ref, v_ref, loads, ga_ref, h_ref, hb_ref,
                  sa, ra, sb, rb, sc, rc, sd, rd, st, rt, lt):
+    dp = dims[6]
     me, grp = lax.axis_index("dp"), lax.axis_index("group")
-    enter(dp, ng, me, grp)
+    arrive = local_loads(((x0_hbm, x0_ref), (g0_hbm, g0_ref), (x1_hbm, x1_ref), (g1_hbm, g1_ref),
+                          (w_hbm, w_ref), (qa_hbm, qa_ref)), loads)
+    greet_all(dp, ng, me, grp)
+    local_grams(dims, arrive, x0_ref, g0_ref, x1_ref, g1_ref, gram_ref, xp_ref, v_ref)
+    all_here(dp, ng)
 
     def copy_a(q):
         to = lax.rem(grp + q, ng)
@@ -190,6 +237,9 @@
     own = pltpu.make_async_copy(rot_ref.at[me], rotin_ref.at[:, me], lt)
     for q in range(1, ng):
         copy_a(q).start()
+    arrive(4)
+    arrive(5)
+    local_rotation(dims, owner_ref, qs_ref, w_ref, qa_ref, rot_ref)
     own.start()
     each(dp, lambda k: copy_t(k).start())
     for q in range(1, ng):
@@ -227,9 +277,10 @@
     own.wait()
 
 
-def coords_kernel(dims, info_ref, gram_ref, rot_ref, qa_ref, qg_ref, qs_ref,
+def coords_kernel(dims, owner_ref, gram_ref, rot_ref, qa_ref, qg_ref, qs_ref,
                   back_ref, fin_ref, fsp_ref, fout_ref, lin_ref, ltap_ref, lout_ref):
-    chans, dp, slots, positions = dims
+    chans, dp, slots, positions, slot_total = dims
+    me = lax.axis_index("dp")
     half = chans // 2
     for l in range(LAYERS):
         base = l * 2 * chans
@@ -243,7 +294,8 @@
         fin_ref[l] = fin / (9.0 * positions[l])
         fout_ref[l] = fout.astype(F32) / (1.0 * positions[l])
         fsp_ref[l] = fsp[0:9, 0:9]
-        qa, qg, qs = qa_ref[info_ref[l]], qg_ref[info_ref[l]], qs_ref[l]
+        slot = owner_ref[l] % slot_total
+        qa, qg, qs = qa_ref[slot], qg_ref[slot], qs_ref[slot]
         prod = jnp.dot(fin.astype(BF16), qa, preferred_element_type=F32)
         lin_ref[l] = jnp.sum(qa.astype(F32) * prod, axis=0, keepdims=True) / (9.0 * positions[l])
         prod = qg.astype(F32) * jnp.dot(fout, qg, preferred_element_type=F32)
@@ -255,7 +307,7 @@
     per = 9 * chans // LANES
     split = chans // LANES
     for s in range(slots):
-        k = jnp.minimum(s * dp + info_ref[4], LAYERS * per - 1)
+        k = jnp.minimum(s * dp + me, LAYERS * per - 1)
         l = k // per
         c = k % per
         lane = lax.broadcasted_iota(jnp.int32, (1, LANES), 1)
@@ -265,16 +317,16 @@
         for piece in range(1, split):
             scale_in = jnp.where(c % split == piece, row[:, piece * LANES:(piece + 1) * LANES],
                                  scale_in)
-        qg = qg_ref[info_ref[l]]
+        qg = qg_ref[owner_ref[l] % slot_total]
         projected = dot_rows(qg, rot_ref[s])
         divisor = (lout_ref[l] * tap) * scale_in + DAMPING
         coords = (projected / divisor).astype(BF16)
         back_ref[s] = jnp.dot(qg, coords, preferred_element_type=F32).astype(BF16)
 
 
-def rows_kernel(dims, info_ref, qs_ref, back_ref, qa_ref, out_ref, in_ref, own_ref, peer_ref,
+def rows_kernel(dims, owner_ref, qs_ref, back_ref, qa_ref, out_ref, in_ref, own_ref, peer_ref,
                 st, rt, lt, sx, rx):
-    dp, ng, rows, chans = dims
+    dp, ng, rows, chans, slot_total = dims
     me, grp = lax.axis_index("dp"), lax.axis_index("group")
     enter(dp, ng, me, grp)
 
@@ -294,8 +346,9 @@
     per = 9 * chans // LANES
     split = chans // LANES
     for l in range(LAYERS):
-        basis = qa_ref[info_ref[l]]
-        mine = info_ref[2 + l] == 1
+        slot = owner_ref[l] % slot_total
+        basis = qa_ref[slot]
+        mine = owner_ref[l] // slot_total == grp
         parts = []
         for t in range(9):
             pieces = []
@@ -304,7 +357,7 @@
                 pieces.append(in_ref[k % dp, k // dp])
             parts.append(jnp.concatenate(pieces, axis=1))
         chan = through_basis(parts, basis, rows, True)
-        turned = mixed_taps(chan, lambda t, u: qs_ref[l, 9 * u + t])
+        turned = mixed_taps(chan, lambda t, u: qs_ref[slot, 9 * u + t])
         for u in range(9):
             value = jnp.where(mine, turned[u], jnp.zeros_like(turned[u]))
             own_ref[l, :, u * chans:(u + 1) * chans] = value.astype(BF16)
@@ -334,44 +387,41 @@
     struct = jax.ShapeDtypeStruct
     dma = pltpu.SemaphoreType.DMA
 
-    local = owner % slot_total
-    holds = (owner // slot_total == lax.axis_index("group")).astype(jnp.int32)
-    info = jnp.concatenate([local, holds, lax.axis_index("dp").astype(jnp.int32)[None]])
-    taps = jnp.stack([lax.dynamic_index_in_dim(basis_spatial, local[l], 0, keepdims=False)
-                      for l in range(LAYERS)]).astype(F32)
-    taps_flat = taps.reshape(LAYERS, 81)
+    taps = basis_spatial.astype(F32)
+    taps_flat = taps.reshape(slot_total, 81)
     taps_wide = jnp.pad(taps, ((0, 0), (0, 7), (0, LANES - 9)))
-
-    gram, rot = pl.pallas_call(
-        functools.partial(local_kernel, (side, outs, (1, 2), images, chans, rows, dp)),
-        out_shape=(struct((gram_rows, chans), BF16), struct((dp, slots, rows, LANES), BF16)),
-        in_specs=[smem, smem] + [vmem] * 6,
-        out_specs=(vmem, vmem),
-        scratch_shapes=[pltpu.VMEM(((side + 2) * side, chans), BF16),
-                        pltpu.VMEM((3, 16, LANES), F32)],
-        compiler_params=pltpu.CompilerParams(vmem_limit_bytes=40 << 20),
-        name="local_terms",
-    )(info, taps_flat, acts_first.reshape(-1, chans), grads_first.reshape(-1, chans),
-      acts_second.reshape(-1, chans), grads_second.reshape(-1, chans), grad_w, basis_in)
+    hbm = pl.BlockSpec(memory_space=pltpu.HBM)
 
     full, rotin = pl.pallas_call(
-        functools.partial(share_kernel, dp, ng),
+        functools.partial(share_kernel, (side, outs, (1, 2), images, chans, rows, dp, slot_total),
+                          ng),
         out_shape=(struct((ng, dp, slice_rows, chans), BF16),
                    struct((slots, dp, rows, LANES), BF16)),
-        in_specs=[vmem, vmem],
+        in_specs=[smem, smem] + [hbm] * 6,
         out_specs=(vmem, vmem),
-        scratch_shapes=[pltpu.VMEM((ng - 1, dp, slice_rows, chans), BF16),
+        scratch_shapes=[pltpu.VMEM((ng, dp, slice_rows, chans), BF16),
+                        pltpu.VMEM((dp, slots, rows, LANES), BF16),
+                        pltpu.VMEM((images * side * side, chans), BF16),
+                        pltpu.VMEM((images * outs[0] * outs[0], chans), BF16),
+                        pltpu.VMEM((images * side * side, chans), BF16),
+                        pltpu.VMEM((images * outs[1] * outs[1], chans), BF16),
+                        pltpu.VMEM(grad_w.shape, BF16),
+                        pltpu.VMEM(basis_in.shape, BF16),
+                        pltpu.VMEM(((side + 2) * side, chans), BF16),
+                        pltpu.VMEM((3, 16, LANES), F32), dma((6, 4)),
+                        pltpu.VMEM((ng - 1, dp, slice_rows, chans), BF16),
                         pltpu.VMEM((dp, slice_rows, chans), BF16),
                         pltpu.VMEM((dp - 1, slice_rows, chans), BF16),
                         dma((ng,)), dma((ng,)), dma((dp,)), dma((dp,)), dma((dp,)), dma((dp,)),
                         dma((ng, dp)), dma((ng, dp)), dma((dp,)), dma((dp,)), dma],
         compiler_params=pltpu.CompilerParams(collective_id=0, has_side_effects=True,
-                                             vmem_limit_bytes=32 << 20),
+                                             vmem_limit_bytes=62 << 20),
         name="share_sums",
-    )(gram.reshape(ng, dp, slice_rows, chans), rot)
+    )(owner, taps_flat, acts_first.reshape(-1, chans), grads_first.reshape(-1, chans),
+      acts_second.reshape(-1, chans), grads_second.reshape(-1, chans), grad_w, basis_in)
 
     back, fin, fsp, fout = pl.pallas_call(
-        functools.partial(coords_kernel, (chans, dp, slots, positions)),
+        functools.partial(coords_kernel, (chans, dp, slots, positions, slot_total)),
         out_shape=(struct((slots, chans, LANES), BF16), struct((LAYERS, chans, chans), F32),
                    struct((LAYERS, 9, 9), F32), struct((LAYERS, chans, chans), F32)),
         in_specs=[smem] + [vmem] * 5,
@@ -380,11 +430,11 @@
                         pltpu.VMEM((LAYERS, chans, LANES), F32)],
         compiler_params=pltpu.CompilerParams(vmem_limit_bytes=32 << 20),
         name="scaled_coords",
-    )(info, full.reshape(gram_rows, chans), rotin.reshape(slots, chans, LANES),
+    )(owner, full.reshape(gram_rows, chans), rotin.reshape(slots, chans, LANES),
       basis_in, basis_out, taps_wide)
 
     precond = pl.pallas_call(
-        functools.partial(rows_kernel, (dp, ng, rows, chans)),
+        functools.partial(rows_kernel, (dp, ng, rows, chans, slot_total)),
         out_shape=struct((LAYERS, rows, 9 * chans), BF16),
         in_specs=[smem, smem, vmem, vmem],
         out_specs=vmem,
@@ -395,7 +445,7 @@
         compiler_params=pltpu.CompilerParams(collective_id=1, has_side_effects=True,
                                              vmem_limit_bytes=32 << 20),
         name="back_rows",
-    )(info, taps_flat, back.reshape(slots, dp, rows, LANES), basis_in)
+    )(owner, taps_flat, back.reshape(slots, dp, rows, LANES), basis_in)
     return precond, fin, fsp, fout
 
 

time: 60.1 us -> 51.8 us (0.86)
  between operations: 4.64 us -> 0.69 us
  local copies, waits for them, and re-layouts: 8.68 us -> 5.22 us
  Pallas kernels: 46.2 us -> 44.9 us
    unnamed x22 -> x14, local copies, waits for them, and re-layouts: 7.9 us -> 4.55 us
    pallas_call x3 -> x2, Pallas kernels: 43.7 us -> 42.4 us  [the longest x1 30.2 us: on_device(): pl.pallas_call(functools.partial(share_kernel, (side, outs, (1, 2), image...]
    convert_element_type x2 -> x1, other arithmetic: 0.02 us -> 0.7 us  [on_device(): taps = basis_spatial.astype(F32)]
    reshape x0 -> x1, local copies, waits for them, and re-layouts: none -> 0.66 us  [on_device(): taps_flat = taps.reshape(slot_total, 81)]
where the time goes in v2:
time: 51.8 us; the launch traced here: 51.5 us
  Pallas kernels  44.9 us (87%)
  local copies, waits for them, and re-layouts  5.22 us (10%)
  other arithmetic  0.7 us (1%)
  between operations  0.69 us (1%)
    pallas_call x1, Pallas kernels, on_device(): pl.pallas_call(functools.partial(share_kernel, (side, outs, (1, 2), image...  30.2 us
    pallas_call x1, Pallas kernels, on_device(): pl.pallas_call(functools.partial(rows_kernel, (dp, ng, rows, chans, slot_...  12.2 us
    unnamed x14, local copies, waits for them, and re-layouts  4.55 us
    pallas_call x1, Pallas kernels, on_device(): pl.pallas_call(functools.partial(coords_kernel, (chans, dp, slots, positi...  2.52 us

profile of v2, /device:TPU:0, one launch (start us, length us, event | category | flops | bytes accessed | tf_op | source)
XLA Modules:
  0.0 51.5 jit_solution(4635154248654352805)
XLA Ops:
  0.6 0.7 %copy_convert_fusion = f32[4,9,9]{2,1,0:T(8,128)S(1)} fusion(bf16[4,9,9]{2,0,1:T(4,128)(2,1)} %param.16), kind=kLoop, calls=%fused_computation | loop fusion | flops 324 | bytes 1944 | tf_op jit(solution)/shard_map/convert_element_type | solution.py:390
  1.3 0.7 %reshape.32.qs_ref = f32[4,81]{1,0:T(4,128)} reshape(f32[4,9,9]{2,1,0:T(8,128)S(1)} %copy_convert_fusion) | data formatting | bytes 2592 | tf_op jit(solution)/shard_map/reshape | solution.py:391
  2.0 0.0 copy-start
  2.0 0.0 copy-start.1
  2.0 30.2 %share_sums.1 = (bf16[2,16,32,256]{3,2,1,0:T(8,128)(2,1)}, bf16[3,16,16,128]{3,2,1,0:T(8,128)(2,1)}) custom-call(s32[2]{0:T(128)} %owner_ref.5, f32[4,81]{1,0:T(4,128)} %reshape.32.qs_ref, bf16[1024,256]{1,0:T(8,128)(2,1)} %bitcast.10, bf16[1024,256]{1,0:T(8,128)(2,1)} %bitcast.11, bf16[1024,256]{1,0:T(8,128)(2,1)} %bitcast.12, bf16[256,256]{1,0:T(8,128)(2,1)} %bitcast.13, ...), custom_call_target="tpu_custom_call" | custom-call | tf_op jit(solution)/shard_map/share_sums/pallas_call | solution.py:395
  32.2 0.0 copy-start.5
  32.3 0.0 copy-done
  32.3 0.0 copy-done.1
  32.3 0.6 %copy-done.5 = s32[2]{0:T(128)S(1)} copy-done((s32[2]{0:T(128)S(1)}, s32[2]{0:T(128)}, u32[]{:S(2)}) %copy-start.5) | copy-done | bytes 32
  32.9 0.0 copy-start.2
  32.9 1.0 %copy-done.2 = bf16[2,16,32,256]{3,2,1,0:T(8,128)(2,1)S(1)} copy-done((bf16[2,16,32,256]{3,2,1,0:T(8,128)(2,1)S(1)}, bf16[2,16,32,256]{3,2,1,0:T(8,128)(2,1)}, u32[]{:S(2)}) %copy-start.2) | copy-done | bytes 524312
  33.9 0.0 copy-start.3
  33.9 0.9 %copy-done.3 = bf16[3,16,16,128]{3,2,1,0:T(8,128)(2,1)S(1)} copy-done((bf16[3,16,16,128]{3,2,1,0:T(8,128)(2,1)S(1)}, bf16[3,16,16,128]{3,2,1,0:T(8,128)(2,1)}, u32[]{:S(2)}) %copy-start.3) | copy-done | bytes 196632
  34.9 2.5 %scaled_coords.1 = (bf16[3,256,128]{2,1,0:T(8,128)(2,1)S(1)}, f32[2,256,256]{2,1,0:T(8,128)}, f32[2,9,9]{2,1,0:T(8,128)S(1)}, f32[2,256,256]{2,1,0:T(8,128)}) custom-call(s32[2]{0:T(128)S(1)} %copy-done.5, bf16[1024,256]{1,0:T(8,128)(2,1)S(1)} %bitcast.7, bf16[3,256,128]{2,1,0:T(8,128)(2,1)S(1)} %bitcast.9, bf16[4,256,256]{2,1,0:T(8,128)(2,1)S(1)} %copy-done, ...), custom_call_target="tpu_custom_call" | custom-call | tf_op jit(solution)/shard_map/scaled_coords/pallas_call | solution.py:423
  37.4 0.0 copy-start.4
  37.4 0.7 %copy-done.4 = f32[4,81]{1,0:T(4,128)S(1)} copy-done((f32[4,81]{1,0:T(4,128)S(1)}, f32[4,81]{1,0:T(4,128)}, u32[]{:S(2)}) %copy-start.4) | copy-done | bytes 1320
  38.1 12.2 %back_rows.1 = bf16[2,16,2304]{2,1,0:T(8,128)(2,1)S(1)} custom-call(s32[2]{0:T(128)S(1)} %copy-done.5, f32[4,81]{1,0:T(4,128)S(1)} %copy-done.4, bf16[3,16,16,128]{3,2,1,0:T(8,128)(2,1)S(1)} %bitcast.8, bf16[4,256,256]{2,1,0:T(8,128)(2,1)S(1)} %copy-done), custom_call_target="tpu_custom_call" | custom-call | tf_op jit(solution)/shard_map/back_rows/pallas_call | solution.py:436
  50.3 0.6 %copy.16 = f32[2,9,9]{2,0,1:T(2,128)} copy(f32[2,9,9]{2,1,0:T(8,128)S(1)} %get-tuple-element.22) | data formatting | bytes 1296
  50.9 0.7 %copy.19 = bf16[2,16,2304]{2,1,0:T(8,128)(2,1)} copy(bf16[2,16,2304]{2,1,0:T(8,128)(2,1)S(1)} %back_rows.1) | data formatting | bytes 294912
  (1 shorter events, 0.0 us)
Async XLA Ops:
  2.0 30.2 %copy-start = (bf16[4,256,256]{2,1,0:T(8,128)(2,1)S(1)}, bf16[4,256,256]{2,1,0:T(8,128)(2,1)}, u32[]{:S(2)}) copy-start(bf16[4,256,256]{2,1,0:T(8,128)(2,1)} %qa_ref.3) | copy-start | bytes 1572868
  2.0 30.3 %copy-start.1 = (bf16[4,256,256]{2,1,0:T(8,128)(2,1)S(1)}, bf16[4,256,256]{2,1,0:T(8,128)(2,1)}, u32[]{:S(2)}) copy-start(bf16[4,256,256]{2,1,0:T(8,128)(2,1)} %qg_ref.1) | copy-start | bytes 1572868
  32.2 0.7 %copy-start.5 = (s32[2]{0:T(128)S(1)}, s32[2]{0:T(128)}, u32[]{:S(2)}) copy-start(s32[2]{0:T(128)} %owner_ref.5) | copy-start | bytes 28
  32.9 1.0 %copy-start.2 = (bf16[2,16,32,256]{3,2,1,0:T(8,128)(2,1)S(1)}, bf16[2,16,32,256]{3,2,1,0:T(8,128)(2,1)}, u32[]{:S(2)}) copy-start(bf16[2,16,32,256]{3,2,1,0:T(8,128)(2,1)} %get-tuple-element.10) | copy-start | bytes 1572868
  33.9 0.9 %copy-start.3 = (bf16[3,16,16,128]{3,2,1,0:T(8,128)(2,1)S(1)}, bf16[3,16,16,128]{3,2,1,0:T(8,128)(2,1)}, u32[]{:S(2)}) copy-start(bf16[3,16,16,128]{3,2,1,0:T(8,128)(2,1)} %get-tuple-element.11) | copy-start | bytes 589828
  37.4 0.7 %copy-start.4 = (f32[4,81]{1,0:T(4,128)S(1)}, f32[4,81]{1,0:T(4,128)}, u32[]{:S(2)}) copy-start(f32[4,81]{1,0:T(4,128)} %reshape.32.qs_ref) | copy-start | bytes 3892

commit v3 on v2

--- a/solution.py
+++ b/solution.py
@@ -110,6 +110,18 @@
         ref[i // dp, i % dp, off:off + step, 0:value.shape[1]] = piece
 
 
+def stacked(pieces):
+    if pieces[0].shape[0] % 16 == 0:
+        return jnp.concatenate(pieces, axis=0)
+    return jnp.concatenate([piece.astype(F32) for piece in pieces], axis=0).astype(BF16)
+
+
+def take_rows(ref, dp, start, count):
+    size = ref.shape[2]
+    first = start // size
+    return stacked([ref[i // dp, i % dp] for i in range(first, first + count // size)])
+
+
 def local_loads(pairs, sems):
     loads = {}
     for i, (src, dst) in enumerate(pairs):
@@ -189,11 +201,6 @@
     pl.semaphore_wait(pltpu.get_barrier_semaphore(), dp + ng - 2)
 
 
-def enter(dp, ng, me, grp):
-    greet_all(dp, ng, me, grp)
-    all_here(dp, ng)
-
-
 def each(n, fn):
     def body(k, c):
         fn(k)
@@ -201,14 +208,14 @@
     lax.fori_loop(1, n, body, 0)
 
 
-def share_kernel(dims, ng, owner_ref, qs_ref, x0_hbm, g0_hbm, x1_hbm, g1_hbm, w_hbm, qa_hbm,
-                 full_ref, rotin_ref, gram_ref, rot_ref, x0_ref, g0_ref, x1_ref, g1_ref, w_ref,
+def share(dims, ng, owner_ref, qs_ref, x0_hbm, g0_hbm, x1_hbm, g1_hbm, w_hbm, qa_hbm,
+                 qg_hbm, full_ref, rotin_ref, qg_ref, gram_ref, rot_ref, x0_ref, g0_ref, x1_ref, g1_ref, w_ref,
                  qa_ref, xp_ref, v_ref, loads, ga_ref, h_ref, hb_ref,
                  sa, ra, sb, rb, sc, rc, sd, rd, st, rt, lt):
     dp = dims[6]
     me, grp = lax.axis_index("dp"), lax.axis_index("group")
     arrive = local_loads(((x0_hbm, x0_ref), (g0_hbm, g0_ref), (x1_hbm, x1_ref), (g1_hbm, g1_ref),
-                          (w_hbm, w_ref), (qa_hbm, qa_ref)), loads)
+                          (w_hbm, w_ref), (qa_hbm, qa_ref), (qg_hbm, qg_ref)), loads)
     greet_all(dp, ng, me, grp)
     local_grams(dims, arrive, x0_ref, g0_ref, x1_ref, g1_ref, gram_ref, xp_ref, v_ref)
     all_here(dp, ng)
@@ -275,21 +282,22 @@
             copy_d(k, q).wait()
     each(dp, finish)
     own.wait()
-
-
-def coords_kernel(dims, owner_ref, gram_ref, rot_ref, qa_ref, qg_ref, qs_ref,
+    arrive(6)
+
+
+def coords_step(dims, owner_ref, gram_ref, rot_ref, qa_ref, qg_ref, qs_ref,
                   back_ref, fin_ref, fsp_ref, fout_ref, lin_ref, ltap_ref, lout_ref):
     chans, dp, slots, positions, slot_total = dims
     me = lax.axis_index("dp")
     half = chans // 2
     for l in range(LAYERS):
         base = l * 2 * chans
-        fin = gram_ref[base:base + chans, :]
+        fin = take_rows(gram_ref, dp, base, chans)
+        fsp = fin[half:half + 16, 0:LANES].astype(F32)
         corner = jnp.transpose(fin[0:half, half:chans].astype(F32))
         low = jnp.concatenate([corner, fin[half:chans, half:chans].astype(F32)], axis=1)
         fin = jnp.concatenate([fin[0:half].astype(F32), low], axis=0)
-        fsp = gram_ref[base + half:base + half + 16, 0:LANES].astype(F32)
-        fout = gram_ref[base + chans:base + 2 * chans, :]
+        fout = take_rows(gram_ref, dp, base + chans, chans)
         fsp = fsp / (1.0 * chans * positions[l])
         fin_ref[l] = fin / (9.0 * positions[l])
         fout_ref[l] = fout.astype(F32) / (1.0 * positions[l])
@@ -318,17 +326,19 @@
             scale_in = jnp.where(c % split == piece, row[:, piece * LANES:(piece + 1) * LANES],
                                  scale_in)
         qg = qg_ref[owner_ref[l] % slot_total]
-        projected = dot_rows(qg, rot_ref[s])
+        projected = dot_rows(qg, stacked([rot_ref[s, e] for e in range(dp)]))
         divisor = (lout_ref[l] * tap) * scale_in + DAMPING
         coords = (projected / divisor).astype(BF16)
-        back_ref[s] = jnp.dot(qg, coords, preferred_element_type=F32).astype(BF16)
-
-
-def rows_kernel(dims, owner_ref, qs_ref, back_ref, qa_ref, out_ref, in_ref, own_ref, peer_ref,
+        back = jnp.dot(qg, coords, preferred_element_type=F32)
+        rows = back_ref.shape[2]
+        for e in range(dp):
+            back_ref[s, e] = back[e * rows:(e + 1) * rows].astype(BF16)
+
+
+def rows_step(dims, owner_ref, qs_ref, back_ref, qa_ref, out_ref, in_ref, own_ref, peer_ref,
                 st, rt, lt, sx, rx):
     dp, ng, rows, chans, slot_total = dims
     me, grp = lax.axis_index("dp"), lax.axis_index("group")
-    enter(dp, ng, me, grp)
 
     def copy_t(k):
         to = lax.rem(me + k, dp)
@@ -371,6 +381,24 @@
     out_ref[...] = total
 
 
+def whole_kernel(dims, ng, slots, positions, *refs):
+    side, outs, strides, images, chans, rows, dp, slot_total = dims
+    owner_ref, qs_ref = refs[0:2]
+    sources = refs[2:9]
+    wide_ref = refs[9]
+    out_ref, fin_ref, fsp_ref, fout_ref = refs[10:14]
+    full_ref, rotin_ref, qg_ref, back_ref = refs[14:18]
+    lin_ref, ltap_ref, lout_ref = refs[18:21]
+    row_scratch = refs[21:29]
+    rest = refs[29:]
+    qa_ref = rest[7]
+    share(dims, ng, owner_ref, qs_ref, *sources, full_ref, rotin_ref, qg_ref, *rest)
+    coords_step((chans, dp, slots, positions, slot_total), owner_ref, full_ref, rotin_ref, qa_ref,
+                qg_ref, wide_ref, back_ref, fin_ref, fsp_ref, fout_ref, lin_ref, ltap_ref, lout_ref)
+    rows_step((dp, ng, rows, chans, slot_total), owner_ref, qs_ref, back_ref, qa_ref, out_ref,
+              *row_scratch)
+
+
 def on_device(dp, ng, acts_first, grads_first, acts_second, grads_second, grad_w, owner,
               basis_in, basis_spatial, basis_out):
     images, side = acts_first.shape[0], acts_first.shape[1]
@@ -392,61 +420,47 @@
     taps_wide = jnp.pad(taps, ((0, 0), (0, 7), (0, LANES - 9)))
     hbm = pl.BlockSpec(memory_space=pltpu.HBM)
 
-    full, rotin = pl.pallas_call(
-        functools.partial(share_kernel, (side, outs, (1, 2), images, chans, rows, dp, slot_total),
-                          ng),
-        out_shape=(struct((ng, dp, slice_rows, chans), BF16),
-                   struct((slots, dp, rows, LANES), BF16)),
-        in_specs=[smem, smem] + [hbm] * 6,
-        out_specs=(vmem, vmem),
-        scratch_shapes=[pltpu.VMEM((ng, dp, slice_rows, chans), BF16),
-                        pltpu.VMEM((dp, slots, rows, LANES), BF16),
-                        pltpu.VMEM((images * side * side, chans), BF16),
-                        pltpu.VMEM((images * outs[0] * outs[0], chans), BF16),
-                        pltpu.VMEM((images * side * side, chans), BF16),
-                        pltpu.VMEM((images * outs[1] * outs[1], chans), BF16),
-                        pltpu.VMEM(grad_w.shape, BF16),
-                        pltpu.VMEM(basis_in.shape, BF16),
-                        pltpu.VMEM(((side + 2) * side, chans), BF16),
-                        pltpu.VMEM((3, 16, LANES), F32), dma((6, 4)),
-                        pltpu.VMEM((ng - 1, dp, slice_rows, chans), BF16),
-                        pltpu.VMEM((dp, slice_rows, chans), BF16),
-                        pltpu.VMEM((dp - 1, slice_rows, chans), BF16),
-                        dma((ng,)), dma((ng,)), dma((dp,)), dma((dp,)), dma((dp,)), dma((dp,)),
-                        dma((ng, dp)), dma((ng, dp)), dma((dp,)), dma((dp,)), dma],
+    dims = (side, outs, (1, 2), images, chans, rows, dp, slot_total)
+    return pl.pallas_call(
+        functools.partial(whole_kernel, dims, ng, slots, positions),
+        out_shape=(struct((LAYERS, rows, 9 * chans), BF16), struct((LAYERS, chans, chans), F32),
+                   struct((LAYERS, 9, 9), F32), struct((LAYERS, chans, chans), F32)),
+        in_specs=[smem, smem] + [hbm] * 7 + [vmem],
+        out_specs=(vmem,) * 4,
+        scratch_shapes=[
+            pltpu.VMEM((ng, dp, slice_rows, chans), BF16),
+            pltpu.VMEM((slots, dp, rows, LANES), BF16),
+            pltpu.VMEM(basis_out.shape, BF16),
+            pltpu.VMEM((slots, dp, rows, LANES), BF16),
+            pltpu.VMEM((LAYERS, 1, chans), F32),
+            pltpu.VMEM((LAYERS, 1, LANES), F32),
+            pltpu.VMEM((LAYERS, chans, LANES), F32),
+            pltpu.VMEM((dp, slots, rows, LANES), BF16),
+            pltpu.VMEM((LAYERS, rows, 9 * chans), BF16),
+            pltpu.VMEM((ng - 1, LAYERS, rows, 9 * chans), BF16),
+            dma((dp,)), dma((dp,)), dma, dma((ng,)), dma((ng,)),
+            pltpu.VMEM((ng, dp, slice_rows, chans), BF16),
+            pltpu.VMEM((dp, slots, rows, LANES), BF16),
+            pltpu.VMEM((images * side * side, chans), BF16),
+            pltpu.VMEM((images * outs[0] * outs[0], chans), BF16),
+            pltpu.VMEM((images * side * side, chans), BF16),
+            pltpu.VMEM((images * outs[1] * outs[1], chans), BF16),
+            pltpu.VMEM(grad_w.shape, BF16),
+            pltpu.VMEM(basis_in.shape, BF16),
+            pltpu.VMEM(((side + 2) * side, chans), BF16),
+            pltpu.VMEM((3, 16, LANES), F32),
+            dma((7, 4)),
+            pltpu.VMEM((ng - 1, dp, slice_rows, chans), BF16),
+            pltpu.VMEM((dp, slice_rows, chans), BF16),
+            pltpu.VMEM((dp - 1, slice_rows, chans), BF16),
+            dma((ng,)), dma((ng,)), dma((dp,)), dma((dp,)), dma((dp,)), dma((dp,)),
+            dma((ng, dp)), dma((ng, dp)), dma((dp,)), dma((dp,)), dma],
         compiler_params=pltpu.CompilerParams(collective_id=0, has_side_effects=True,
                                              vmem_limit_bytes=62 << 20),
-        name="share_sums",
+        name="precondition",
     )(owner, taps_flat, acts_first.reshape(-1, chans), grads_first.reshape(-1, chans),
-      acts_second.reshape(-1, chans), grads_second.reshape(-1, chans), grad_w, basis_in)
-
-    back, fin, fsp, fout = pl.pallas_call(
-        functools.partial(coords_kernel, (chans, dp, slots, positions, slot_total)),
-        out_shape=(struct((slots, chans, LANES), BF16), struct((LAYERS, chans, chans), F32),
-                   struct((LAYERS, 9, 9), F32), struct((LAYERS, chans, chans), F32)),
-        in_specs=[smem] + [vmem] * 5,
-        out_specs=(vmem,) * 4,
-        scratch_shapes=[pltpu.VMEM((LAYERS, 1, chans), F32), pltpu.VMEM((LAYERS, 1, LANES), F32),
-                        pltpu.VMEM((LAYERS, chans, LANES), F32)],
-        compiler_params=pltpu.CompilerParams(vmem_limit_bytes=32 << 20),
-        name="scaled_coords",
-    )(owner, full.reshape(gram_rows, chans), rotin.reshape(slots, chans, LANES),
-      basis_in, basis_out, taps_wide)
-
-    precond = pl.pallas_call(
-        functools.partial(rows_kernel, (dp, ng, rows, chans, slot_total)),
-        out_shape=struct((LAYERS, rows, 9 * chans), BF16),
-        in_specs=[smem, smem, vmem, vmem],
-        out_specs=vmem,
-        scratch_shapes=[pltpu.VMEM((dp, slots, rows, LANES), BF16),
-                        pltpu.VMEM((LAYERS, rows, 9 * chans), BF16),
-                        pltpu.VMEM((ng - 1, LAYERS, rows, 9 * chans), BF16),
-                        dma((dp,)), dma((dp,)), dma, dma((ng,)), dma((ng,))],
-        compiler_params=pltpu.CompilerParams(collective_id=1, has_side_effects=True,
-                                             vmem_limit_bytes=32 << 20),
-        name="back_rows",
-    )(owner, taps_flat, back.reshape(slots, dp, rows, LANES), basis_in)
-    return precond, fin, fsp, fout
+      acts_second.reshape(-1, chans), grads_second.reshape(-1, chans), grad_w, basis_in,
+      basis_out, taps_wide)
 
 
 def solution(mesh):

time: 51.8 us -> 49.1 us (0.948)
  Pallas kernels: 44.9 us -> 40.6 us
  local copies, waits for them, and re-layouts: 5.22 us -> 6.91 us
    pallas_call x3 -> x1, Pallas kernels: 44.9 us -> 40.6 us  [on_device(): pl.pallas_call(functools.partial(whole_kernel, dims, ng, slots, positions...]
    pallas_call x0 -> x1, local copies, waits for them, and re-layouts: none -> 1.32 us  [on_device(): pl.pallas_call(functools.partial(whole_kernel, dims, ng, slots, positions...]
    pad x1, local copies, waits for them, and re-layouts: 0.01 us -> 0.62 us  [on_device(): taps_wide = jnp.pad(taps, ((0, 0), (0, 7), (0, LANES - 9)))]
    unnamed x14 -> x5, local copies, waits for them, and re-layouts: 4.55 us -> 4.3 us
where the time goes in v3:
time: 49.1 us; the launch traced here: 48.8 us
  Pallas kernels  40.6 us (83%)
  local copies, waits for them, and re-layouts  6.91 us (14%)
  other arithmetic  0.7 us (1%)
  between operations  0.64 us (1%)
    pallas_call x1, Pallas kernels, on_device(): pl.pallas_call(functools.partial(whole_kernel, dims, ng, slots, positions...  40.6 us
    unnamed x5, local copies, waits for them, and re-layouts  4.3 us
    pallas_call x1, local copies, waits for them, and re-layouts, on_device(): pl.pallas_call(functools.partial(whole_kernel, dims, ng, slots, positions...  1.32 us

profile of v3, /device:TPU:0, one launch (start us, length us, event | category | flops | bytes accessed | tf_op | source)
XLA Modules:
  0.0 48.8 jit_solution(9620056319725624265)
XLA Ops:
  0.6 0.7 %copy_convert_fusion = f32[4,9,9]{2,1,0:T(8,128)S(1)} fusion(bf16[4,9,9]{2,0,1:T(4,128)(2,1)} %param.16), kind=kLoop, calls=%fused_computation | loop fusion | flops 324 | bytes 1944 | tf_op jit(solution)/shard_map/convert_element_type | solution.py:418
  1.3 0.7 %reshape.23.refs_1_ = f32[4,81]{1,0:T(4,128)} reshape(f32[4,9,9]{2,1,0:T(8,128)S(1)} %copy_convert_fusion) | data formatting | bytes 2592 | tf_op jit(solution)/shard_map/reshape | solution.py:419
  2.0 0.6 %pad.4.refs_9_ = f32[4,16,128]{2,1,0:T(8,128)} pad(f32[4,9,9]{2,1,0:T(8,128)S(1)} %copy_convert_fusion, f32[]{:T(128)} %constant.2.clone.1), padding=0_0x0_7x0_119 | pad | bytes 34068 | tf_op jit(solution)/shard_map/jit(_pad)/pad | solution.py:420
  2.6 40.6 %precondition.1 = (bf16[2,16,2304]{2,1,0:T(8,128)(2,1)}, f32[2,256,256]{2,1,0:T(8,128)}, f32[2,9,9]{2,1,0:T(8,128)}, f32[2,256,256]{2,1,0:T(8,128)}) custom-call(s32[2]{0:T(128)} %refs_0_.1, f32[4,81]{1,0:T(4,128)} %reshape.23.refs_1_, bf16[1024,256]{1,0:T(8,128)(2,1)} %bitcast.4, bf16[1024,256]{1,0:T(8,128)(2,1)} %bitcast.5, bf16[1024,256]{1,0:T(8,128)(2,1)} %bitcast.6, ...), custom_call_target="tpu_custom_call" | custom-call | tf_op jit(solution)/shard_map/precondition/pallas_call | solution.py:424
  43.2 1.3 %copy.16 = f32[2,9,9]{2,0,1:T(2,128)} copy(f32[2,9,9]{2,1,0:T(8,128)} %get-tuple-element.10) | data formatting | bytes 1296 | tf_op jit(solution)/shard_map/precondition/pallas_call | solution.py:424
  44.5 1.6 %copy.21 = bf16[2,16,2304]{2,1,0:T(8,128)(2,1)} copy(bf16[2,16,2304]{2,1,0:T(8,128)(2,1)} %get-tuple-element.16) | data formatting | bytes 294912
  46.1 0.0 copy-start
  46.1 1.9 %copy.22 = f32[2,256,256]{2,1,0:T(8,128)} copy(f32[2,256,256]{2,1,0:T(8,128)} %get-tuple-element.17) | data formatting | bytes 1048576
  48.0 0.0 copy-done
  48.0 0.8 %copy.23 = f32[2,256,256]{2,1,0:T(8,128)} copy(f32[2,256,256]{2,1,0:T(8,128)S(1)} %copy-done) | data formatting | bytes 1048576
Async XLA Ops:
  46.1 1.9 %copy-start = (f32[2,256,256]{2,1,0:T(8,128)S(1)}, f32[2,256,256]{2,1,0:T(8,128)}, u32[]{:S(2)}) copy-start(f32[2,256,256]{2,1,0:T(8,128)} %get-tuple-element.19) | copy-start | bytes 1572868
